TPU v7x, 256 devices: a whole 4x4x8 slice. The times are simulated.
256 devices in a mesh: row: 8 (over z), col: 32 (over x, y, core).
Axes of the slice: x: 4, y: 4, z: 8, core: 2. Of those that a mesh axis runs over, the one named last changes fastest.
Arguments:
- h_values: float32 [8, 512, 4096], P('row', 'col'), as said below
- h_places: int32 [8, 512], P('row', 'col'), may hold values from 0 to 15, as said below
- h_counts: int32 [8, 32], P('row', 'col'), may hold values from 0 to 16, as said below
- p_values: float32 [8, 512, 4096], P('row', 'col'), as said below
- p_places: int32 [8, 512], P('row', 'col'), may hold values from 0 to 15, as said below
- p_counts: int32 [8, 32], P('row', 'col'), may hold values from 0 to 16, as said below
- s_values: float32 [8, 512, 4096], P('row', 'col'), as said below
- s_places: int32 [8, 512], P('row', 'col'), may hold values from 0 to 15, as said below
- s_counts: int32 [8, 32], P('row', 'col'), may hold values from 0 to 16, as said below
- x_places: int32 [8, 512], P('row', 'col'), may hold values from 0 to 15, as said below
- x_counts: int32 [8, 32], P('row', 'col'), may hold values from 0 to 16, as said below
Outputs:
- gradient: float32 [8, 512, 4096], P('row', 'col')
Inputs may be any that keep to these rules, and one draw needn't show every extreme that they name: `h_places`: in each tile the 16 entries are a permutation of the tile's positions; the first count entries are the present blocks. Every pattern is symmetric, holds every block whose block row and block column lie in the same row panel, and every block (i, j) whose cyclic block distance min(|i - j|, 64 - |i - j|) is 2 or less or exactly 32. `p_places`: as for h_places. `s_places`: as for h_places. `x_places`: as for h_places. `h_counts`: every tile whose block columns lie in its own row panel is full. `p_counts`: as for h_counts. `s_counts`: as for h_counts. `x_counts`: as for h_counts. `h_values`: the assembled H is symmetric. `p_values`: the assembled P is symmetric. `s_values`: the assembled S is symmetric.
All inputs are finite; a program needn't handle non-finite values.
Results may differ from a plain program's by a relative error of at most 0.000088.
Values sent between devices are 32-bit elements; how exact they have to be, the bound alone decides.
A program may use at most 64 MiB of HBM per device.

v0:
```python
import jax
import jax.numpy as jnp
from jax import lax
from jax.sharding import PartitionSpec as P

BS = 64
TC = 2


def from_root(value, axis, source):
    kept = jnp.where(lax.axis_index(axis) == source, value, 0).astype(value.dtype)
    return lax.psum(kept, axis)


def assemble(values, places, counts):
    blocks_in = values[0]
    capacity = blocks_in.shape[0]
    slot_ids = lax.iota(jnp.int32, capacity)
    matches = (places[0][:, None] == slot_ids[None, :]) & (slot_ids[:, None] < counts[0, 0])
    spread = jnp.dot(matches.astype(jnp.float32).T, blocks_in, precision=lax.Precision.HIGHEST)
    row_count = capacity // TC
    return (
        spread.reshape(row_count, TC, BS, BS).transpose(0, 2, 1, 3).reshape(row_count * BS, TC * BS)
    )


def expand_mask(present, row_count, col_count):
    flags = present.reshape(row_count, col_count)
    return jnp.broadcast_to(flags[:, None, :, None], (row_count, BS, col_count, BS)).reshape(
        row_count * BS, col_count * BS
    )


def tile_mask(places, counts):
    capacity = places.shape[1]
    slot_ids = lax.iota(jnp.int32, capacity)
    matches = (places[0][:, None] == slot_ids[None, :]) & (slot_ids[:, None] < counts[0, 0])
    present = jnp.sum(matches.astype(jnp.float32), axis=0)
    return expand_mask(present, capacity // TC, TC)


def tile_to_slots(tile, places, counts):
    row_count = tile.shape[0] // BS
    blocks = (
        tile.reshape(row_count, BS, TC, BS).transpose(0, 2, 1, 3).reshape(row_count * TC, BS * BS)
    )
    picked = jnp.take(blocks, places[0], axis=0)
    slot_ids = lax.iota(jnp.int32, places.shape[1])
    used = (slot_ids < counts[0, 0]).astype(jnp.float32)
    return (picked * used[:, None])[None]


def shards(
    h_values,
    h_places,
    h_counts,
    p_values,
    p_places,
    p_counts,
    s_values,
    s_places,
    s_counts,
    x_places,
    x_counts,
):
    col_index = lax.axis_index("col")
    h_tile = assemble(h_values, h_places, h_counts)
    p_tile = assemble(p_values, p_places, p_counts)
    s_tile = assemble(s_values, s_places, s_counts)
    mask_tile = tile_mask(x_places, x_counts)
    row_width = h_tile.shape[0]
    col_width = h_tile.shape[1]
    p_columns, s_columns = (
        lax.all_gather(p_tile, "row", axis=0, tiled=True),
        lax.all_gather(s_tile, "row", axis=0, tiled=True),
    )
    product = jnp.dot(
        lax.all_gather(h_tile, "col", axis=1, tiled=True),
        p_columns,
        precision=lax.Precision.HIGHEST,
    )
    y_tile = mask_tile * product
    y_panel = lax.all_gather(y_tile, "col", axis=1, tiled=True)
    x_tile = mask_tile * jnp.dot(y_panel, s_columns, precision=lax.Precision.HIGHEST)
    per_panel = row_width // col_width
    source_row = col_index // per_panel
    offset = col_index % per_panel * col_width
    y_part = lax.dynamic_slice_in_dim(y_panel, offset, col_width, 0)
    y_mirror = from_root(y_part, "row", source_row)
    far_part = lax.dot_general(
        lax.all_gather(s_tile, "col", axis=1, tiled=True),
        y_mirror,
        (((1,), (1,)), ((), ())),
        precision=lax.Precision.HIGHEST,
    )
    mirrored = mask_tile * far_part
    return tile_to_slots(x_tile + mirrored, x_places, x_counts)


def solution(mesh):
    in_specs = (
        P("row", "col", None),
        P("row", "col"),
        P("row", "col"),
        P("row", "col", None),
        P("row", "col"),
        P("row", "col"),
        P("row", "col", None),
        P("row", "col"),
        P("row", "col"),
        P("row", "col"),
        P("row", "col"),
    )
    out_specs = P("row", "col", None)
    return jax.shard_map(shards, mesh=mesh, in_specs=in_specs, out_specs=out_specs, check_vma=False)
```

profile of v0, /device:TPU:2, one launch (start us, length us, event | category | flops | bytes accessed | tf_op | source)
XLA Modules:
  0.0 405.1 jit_solution(8840308818379448259)
XLA Ops:
  6.5 0.0 copy-start
  6.5 0.0 all-gather.8.cloned.1.call-start
  7.3 1.1 dot_general.34
  8.4 0.0 copy-start.2
  8.4 1.3 convolution_bitcast_fusion.1
  9.8 0.3 copy.26
  10.0 0.9 reshape.190
  10.9 0.0 copy-start.4
  10.9 0.0 all-gather.8.cloned.1.call-update
  10.9 0.0 all-gather.6.cloned.1.call-start
  11.6 0.0 copy-done
  11.6 0.2 dot_general.31
  11.9 0.0 copy-done.2
  11.9 0.7 convolution_bitcast_fusion.2
  12.6 0.3 copy.24
  12.8 0.9 reshape.189
  13.7 0.0 all-gather.6.cloned.1.call-update
  13.7 0.0 all-gather.10.cloned.1.call-start
  14.4 0.0 copy-done.4
  14.4 0.1 convert_reduce_fusion
  14.5 0.1 broadcast_in_dim.19
  14.6 0.2 broadcast_in_dim.20
  14.8 0.3 reshape.188
  15.1 0.0 copy-start.1
  15.2 0.0 copy-start.3
  15.2 40.0 %all-gather.8.cloned.1.call-done = f32[4096,128]{0,1:T(8,128)} async-done(((f32[512,128]{0,1:T(8,128)}), f32[4096,128]{0,1:T(8,128)}) %all-gather.8.cloned.1.call-update) | async-done | bytes 2097168 | tf_op jit(solution)/shard_map/all_gather | solution.py:74
  55.1 59.1 %all-gather.6.cloned.1.call-done = f32[512,4096]{0,1:T(8,128)} async-done(((f32[512,128]{0,1:T(8,128)}), f32[512,4096]{0,1:T(8,128)}) %all-gather.6.cloned.1.call-update) | async-done | bytes 8388624 | tf_op jit(solution)/shard_map/all_gather | solution.py:78
  114.2 16.5 %convolution_multiply_fusion = f32[512,128]{1,0:T(8,128)} fusion(f32[512,128]{1,0:T(8,128)S(1)} %reshape.188, f32[512,4096]{0,1:T(8,128)} %all-gather.6.cloned.1.call-done, f32[4096,128]{0,1:T(8,128)} %all-gather.8.cloned.1.call-done), kind=kOutput, calls=%fused_computation.7 | convolution fusion | flops 3221291008 | bytes 11010048 | tf_op jit(solution)/shard_map/dot_general | solution.py:77
  130.7 0.0 all-gather.10.cloned.1.call-update
  130.8 0.0 all-gather.12.cloned.1.call-start
  131.4 0.0 copy-done.1
  131.5 0.2 dot_general.38
  131.7 0.0 copy-done.3
  131.7 0.7 convolution_bitcast_fusion
  132.4 0.3 copy.28
  132.7 0.9 reshape.191
  133.5 0.0 all-gather.12.cloned.1.call-update
  133.6 0.0 all-gather.14.cloned.1.call-start
  133.6 0.5 all-gather.14.cloned.1.call-update
  134.2 0.2 all-reduce.2.cloned.1.call-start
  134.4 60.4 %all-gather.10.cloned.1.call-done = f32[512,4096]{1,0:T(8,128)} async-done(((f32[512,128]{1,0:T(8,128)}), f32[512,4096]{1,0:T(8,128)}) %all-gather.10.cloned.1.call-update) | async-done | bytes 8388624 | tf_op jit(solution)/shard_map/all_gather | solution.py:83
  194.8 3.2 dynamic-slice_select_fusion
  198.0 0.0 all-reduce.2.cloned.1.call-update
  198.0 39.7 %all-gather.12.cloned.1.call-done = f32[4096,128]{0,1:T(8,128)} async-done(((f32[512,128]{0,1:T(8,128)}), f32[4096,128]{0,1:T(8,128)}) %all-gather.12.cloned.1.call-update) | async-done | bytes 2097168 | tf_op jit(solution)/shard_map/all_gather | solution.py:75
  237.7 9.3 %fusion.29 = f32[512,128]{1,0:T(8,128)S(1)} fusion(f32[512,4096]{1,0:T(8,128)} %all-gather.10.cloned.1.call-done, f32[4096,128]{0,1:T(8,128)} %all-gather.12.cloned.1.call-done), kind=kOutput, calls=%fused_computation.48 | convolution fusion | flops 3221225472 | bytes 10747904 | tf_op jit(solution)/shard_map/dot_general | solution.py:84
  247.0 49.5 %all-gather.14.cloned.1.call-done = f32[512,4096]{0,1:T(8,128)} async-done(((f32[512,128]{0,1:T(8,128)}), f32[512,4096]{0,1:T(8,128)}) %all-gather.14.cloned.1.call-update) | async-done | bytes 8388624 | tf_op jit(solution)/shard_map/all_gather | solution.py:91
  296.6 83.7 %all-reduce.2.cloned.1.call-done = f32[128,4096]{1,0:T(8,128)} async-done(((f32[128,4096]{1,0:T(8,128)}), f32[128,4096]{1,0:T(8,128)}) %all-reduce.2.cloned.1.call-update) | async-done | bytes 2097168 | tf_op jit(solution)/shard_map/psum | solution.py:12
  380.3 16.0 %fusion = f32[512,128]{1,0:T(8,128)S(1)} fusion(f32[512,128]{1,0:T(8,128)S(1)} %reshape.188, f32[512,128]{1,0:T(8,128)S(1)} %fusion.29, f32[512,4096]{0,1:T(8,128)} %all-gather.14.cloned.1.call-done, f32[128,4096]{1,0:T(8,128)} %all-reduce.2.cloned.1.call-done), kind=kOutput, calls=%fused_computation.6 | convolution fusion | flops 3221356544 | bytes 11272192 | tf_op jit(solution)/shard_map/dot_general | solution.py:90
  396.3 0.3 reshape.192
  396.7 0.2 reshape.193
  396.9 0.6 gather_fusion
  397.5 0.8 fusion.7
  (9 shorter events, 0.1 us)
Async XLA Ops:
  6.5 5.1 %copy-start = (f32[1,16,4096]{2,1,0:T(8,128)S(1)}, f32[1,16,4096]{2,1,0:T(8,128)}, u32[]{:S(2)}) copy-start(f32[1,16,4096]{2,1,0:T(8,128)} %param.11) | copy-start | bytes 786436
  6.5 48.6 %all-gather.8.cloned.1.call-start = ((), (), s32[]{:S(2)}) async-start(), calls=%async_computation.1 | async-start | bytes 2359296 | tf_op jit(solution)/shard_map/all_gather | solution.py:74
  8.4 3.5 copy-start.2
  10.9 3.5 copy-start.4
  10.9 103.3 %all-gather.6.cloned.1.call-start = ((), (), s32[]{:S(2)}) async-start(), calls=%async_computation | async-start | bytes 8650752 | tf_op jit(solution)/shard_map/all_gather | solution.py:78
  13.7 181.1 %all-gather.10.cloned.1.call-start = ((), (), s32[]{:S(2)}) async-start(), calls=%async_computation.2 | async-start | bytes 8650752 | tf_op jit(solution)/shard_map/all_gather | solution.py:83
  15.1 116.3 %copy-start.1 = (f32[1,16,4096]{2,1,0:T(8,128)S(1)}, f32[1,16,4096]{2,1,0:T(8,128)}, u32[]{:S(2)}) copy-start(f32[1,16,4096]{2,1,0:T(8,128)} %param.17) | copy-start | bytes 786436
  15.2 116.5 %copy-start.3 = (s32[1,16]{1,0:T(1,128)S(1)}, s32[1,16]{1,0:T(1,128)}, u32[]{:S(2)}) copy-start(s32[1,16]{1,0:T(1,128)} %param.18) | copy-start | bytes 196
  130.8 106.9 %all-gather.12.cloned.1.call-start = ((), (), s32[]{:S(2)}) async-start(), calls=%async_computation.3 | async-start | bytes 2359296 | tf_op jit(solution)/shard_map/all_gather | solution.py:75
  133.6 163.0 %all-gather.14.cloned.1.call-start = ((), (), s32[]{:S(2)}) async-start(), calls=%async_computation.4 | async-start | bytes 8650752 | tf_op jit(solution)/shard_map/all_gather | solution.py:91
  134.2 246.2 %all-reduce.2.cloned.1.call-start = ((), (), s32[]{:S(2)}) async-start(), calls=%async_computation.5 | async-start | bytes 4194304 | tf_op jit(solution)/shard_map/psum | solution.py:12
Sparse Core Ops, SparseCore 0:
  11.1 44.0 all-gather.7
  57.7 56.4 all-gather.5
  130.9 63.8 all-gather.9
  196.5 41.1 all-gather.11
  240.1 56.4 all-gather.13
  298.8 81.4 all-reduce.1
where the time goes:
time: 405 us
  waiting for transfers between devices  333 us (82%)
  matrix products  44.6 us (11%)
  between operations  16.4 us (4%)
  local copies, waits for them, and re-layouts  6.76 us (2%)
  other arithmetic  4.09 us (1%)
    psum x1, waiting for transfers between devices, from_root(): return lax.psum(kept, axis)  83.7 us
    all_gather x1, waiting for transfers between devices, shards(): y_panel = lax.all_gather(y_tile, 'col', axis=1, tiled=True)  60.4 us
    all_gather x1, waiting for transfers between devices, shards(): lax.all_gather(h_tile, 'col', axis=1, tiled=True)  59.1 us
    all_gather x1, waiting for transfers between devices, shards(): lax.all_gather(s_tile, 'col', axis=1, tiled=True)  49.5 us
    all_gather x1, waiting for transfers between devices, shards(): lax.all_gather(p_tile, 'row', axis=0, tiled=True)  40 us
    all_gather x1, waiting for transfers between devices, shards(): lax.all_gather(s_tile, 'row', axis=0, tiled=True)  39.7 us
    dot_general x1, matrix products, shards(): jnp.dot(lax.all_gather(h_tile, 'col', axis=1, tiled=True), p_columns, pre...  16.5 us
    dot_general x1, matrix products, shards(): lax.dot_general(lax.all_gather(s_tile, 'col', axis=1, tiled=True), y_mirr...  16 us
  transfers between devices with their start and end apart: 6, of which 6 were waited for; matrix products, arithmetic and copies ran while one was open for 4% of the time, Pallas kernels for 0%

commit v1 on v0

--- a/solution.py
+++ b/solution.py
@@ -80,7 +80,9 @@
         precision=lax.Precision.HIGHEST,
     )
     y_tile = mask_tile * product
-    y_panel = lax.all_gather(y_tile, "col", axis=1, tiled=True)
+    y_panel = jnp.concatenate(
+        lax.all_to_all(jnp.stack([y_tile] * lax.axis_size("col")), "col", 0, 0), axis=1
+    )
     x_tile = mask_tile * jnp.dot(y_panel, s_columns, precision=lax.Precision.HIGHEST)
     per_panel = row_width // col_width
     source_row = col_index // per_panel

time: 405 us -> 397 us (0.980)
  waiting for transfers between devices: 333 us -> 309 us
  matrix products: 44.6 us -> 50.6 us
  starting transfers between devices: 0.39 us -> 6.01 us
  local copies, waits for them, and re-layouts: 6.76 us -> 11.2 us
    all_to_all x0 -> x1, waiting for transfers between devices: none -> 111 us  [shards(): lax.all_to_all(jnp.stack([y_tile] * lax.axis_size('col')), 'col', 0, 0)]
    all_gather x1 -> x0, waiting for transfers between devices: 60.4 us -> none  [shards(): y_panel = lax.all_gather(y_tile, 'col', axis=1, tiled=True)]
    all_gather x1, waiting for transfers between devices: 49.5 us -> 0.08 us  [shards(): lax.all_gather(s_tile, 'col', axis=1, tiled=True)]
    all_gather x1, waiting for transfers between devices: 39.7 us -> 0.02 us  [shards(): lax.all_gather(s_tile, 'row', axis=0, tiled=True)]
    psum x1, waiting for transfers between devices: 83.7 us -> 102 us  [from_root(): return lax.psum(kept, axis)]
    dot_general x1, matrix products: 9.35 us -> 16.1 us  [shards(): jnp.dot(y_panel, s_columns, precision=lax.Precision.HIGHEST)]
    all_to_all x0 -> x1, starting transfers between devices: none -> 5.84 us  [shards(): lax.all_to_all(jnp.stack([y_tile] * lax.axis_size('col')), 'col', 0, 0)]
    another operation x0 -> x1, local copies, waits for them, and re-layouts: none -> 4.3 us  [shards(): jnp.stack([y_tile] * lax.axis_size('col'))]
  transfers between devices with their start and end apart: 6 -> 6, of which waited for: 6 -> 5; matrix products, arithmetic and copies ran while one was open for 4% -> 11% of each run, Pallas kernels for 0% -> 0%
where the time goes in v1:
time: 397 us
  waiting for transfers between devices  309 us (78%)
  matrix products  50.6 us (13%)
  between operations  16 us (4%)
  local copies, waits for them, and re-layouts  11.2 us (3%)
  starting transfers between devices  6.01 us (2%)
  other arithmetic  4.06 us (1%)
    all_to_all x1, waiting for transfers between devices, shards(): lax.all_to_all(jnp.stack([y_tile] * lax.axis_size('col')), 'col', 0, 0)  111 us
    psum x1, waiting for transfers between devices, from_root(): return lax.psum(kept, axis)  102 us
    all_gather x1, waiting for transfers between devices, shards(): lax.all_gather(h_tile, 'col', axis=1, tiled=True)  59.1 us
    all_gather x1, waiting for transfers between devices, shards(): lax.all_gather(p_tile, 'row', axis=0, tiled=True)  36.6 us
    dot_general x1, matrix products, shards(): jnp.dot(y_panel, s_columns, precision=lax.Precision.HIGHEST)  16.1 us
    dot_general x1, matrix products, shards(): lax.dot_general(lax.all_gather(s_tile, 'col', axis=1, tiled=True), y_mirr...  16 us
    dot_general x1, matrix products, shards(): jnp.dot(lax.all_gather(h_tile, 'col', axis=1, tiled=True), p_columns, pre...  15.8 us
  transfers between devices with their start and end apart: 6, of which 5 were waited for; matrix products, arithmetic and copies ran while one was open for 11% of the time, Pallas kernels for 0%

profile of v1, /device:TPU:2, one launch (start us, length us, event | category | flops | bytes accessed | tf_op | source)
XLA Modules:
  0.0 396.8 jit_solution(16011420224244355452)
XLA Ops:
  6.5 0.0 copy-start
  6.5 0.0 all-gather.7.cloned.1.call-start
  6.5 1.2 dot_general.34
  7.7 0.0 copy-start.2
  8.4 1.3 convolution_bitcast_fusion.1
  9.8 0.3 copy.27
  10.0 0.9 reshape.198
  10.9 0.0 copy-start.1
  10.9 0.0 all-gather.7.cloned.1.call-update
  10.9 0.0 all-gather.5.cloned.1.call-start
  11.0 0.0 copy-done
  11.0 0.2 dot_general.31
  11.2 0.0 copy-start.3
  11.9 0.0 copy-done.2
  11.9 0.7 convolution_bitcast_fusion.2
  12.6 0.3 copy.25
  12.9 0.9 reshape.197
  13.7 0.0 all-gather.5.cloned.1.call-update
  13.7 0.0 all-gather.9.cloned.1.call-start
  13.8 0.0 copy-done.1
  13.8 0.0 copy-start.4
  13.8 0.2 dot_general.38
  14.7 0.0 copy-done.3
  14.7 0.7 convolution_bitcast_fusion
  15.4 0.3 copy.30
  15.7 0.9 reshape.201
  16.6 0.0 all-gather.9.cloned.1.call-update
  16.6 0.0 all-gather.11.cloned.1.call-start
  16.6 0.5 all-gather.11.cloned.1.call-update
  17.8 0.0 copy-done.4
  17.8 0.1 convert_reduce_fusion
  17.9 0.1 broadcast_in_dim.19
  18.0 0.2 broadcast_in_dim.20
  18.2 0.3 reshape.196
  18.5 36.6 %all-gather.7.cloned.1.call-done = f32[4096,128]{0,1:T(8,128)} async-done(((f32[512,128]{0,1:T(8,128)}), f32[4096,128]{0,1:T(8,128)}) %all-gather.7.cloned.1.call-update) | async-done | bytes 2097168 | tf_op jit(solution)/shard_map/all_gather | solution.py:74
  55.1 59.1 %all-gather.5.cloned.1.call-done = f32[512,4096]{0,1:T(8,128)} async-done(((f32[512,128]{0,1:T(8,128)}), f32[512,4096]{0,1:T(8,128)}) %all-gather.5.cloned.1.call-update) | async-done | bytes 8388624 | tf_op jit(solution)/shard_map/all_gather | solution.py:78
  114.2 15.8 %convolution_multiply_fusion = f32[512,128]{1,0:T(8,128)S(1)} fusion(f32[512,128]{1,0:T(8,128)S(1)} %reshape.196, f32[512,4096]{0,1:T(8,128)} %all-gather.5.cloned.1.call-done, f32[4096,128]{0,1:T(8,128)} %all-gather.7.cloned.1.call-done), kind=kOutput, calls=%fused_computation.7 | convolution fusion | flops 3221291008 | bytes 11010048 | tf_op jit(solution)/shard_map/dot_general | solution.py:77
  130.0 0.1 copy.28
  130.2 4.3 %stack.2 = f32[32,512,128]{1,2,0:T(8,128)} broadcast(f32[512,128]{0,1:T(8,128)S(1)} %copy.28), dimensions={1,2} | broadcast | bytes 8650752 | tf_op jit(solution)/shard_map/stack | solution.py:84
  134.5 5.8 %all-to-all-start = ((f32[32,512,128]{1,2,0:T(8,128)}), f32[32,512,128]{1,2,0:T(8,128)}, u32[]{:S(2)}, u32[]{:S(2)}) async-start(f32[32,512,128]{1,2,0:T(8,128)} %stack.2), calls=%async_computation | async-start | bytes 16777216 | tf_op jit(solution)/shard_map/all_to_all | solution.py:84
  140.3 0.0 all-reduce.2.cloned.1.call-start
  140.4 110.8 %all-to-all-done = f32[32,512,128]{1,2,0:T(8,128)} async-done(((f32[32,512,128]{1,2,0:T(8,128)}), f32[32,512,128]{1,2,0:T(8,128)}, u32[]{:S(2)}, u32[]{:S(2)}) %all-to-all-start) | async-done | bytes 8388640 | tf_op jit(solution)/shard_map/all_to_all | solution.py:84
  251.2 3.1 dynamic-slice_select_fusion
  254.3 0.0 all-reduce.2.cloned.1.call-update
  254.4 0.0 all-gather.9.cloned.1.call-done
  254.4 16.1 %fusion.29 = f32[512,128]{1,0:T(8,128)S(1)} fusion(f32[512,4096]{0,1:T(8,128)} %bitcast.19, f32[4096,128]{0,1:T(8,128)} %all-gather.9.cloned.1.call-done), kind=kOutput, calls=%fused_computation.48 | convolution fusion | flops 3221225472 | bytes 10747904 | tf_op jit(solution)/shard_map/dot_general | solution.py:86
  270.5 0.1 all-gather.11.cloned.1.call-done
  270.5 101.8 %all-reduce.2.cloned.1.call-done = f32[128,4096]{0,1:T(8,128)} async-done(((f32[128,4096]{0,1:T(8,128)}), f32[128,4096]{0,1:T(8,128)}) %all-reduce.2.cloned.1.call-update) | async-done | bytes 2097168 | tf_op jit(solution)/shard_map/psum | solution.py:12
  372.3 16.0 %fusion = f32[512,128]{1,0:T(8,128)S(1)} fusion(f32[512,128]{1,0:T(8,128)S(1)} %reshape.196, f32[512,128]{1,0:T(8,128)S(1)} %fusion.29, f32[512,4096]{0,1:T(8,128)} %all-gather.11.cloned.1.call-done, f32[128,4096]{0,1:T(8,128)} %all-reduce.2.cloned.1.call-done), kind=kOutput, calls=%fused_computation.6 | convolution fusion | flops 3221356544 | bytes 11272192 | tf_op jit(solution)/shard_map/dot_general | solution.py:92
  388.3 0.3 reshape.202
  388.7 0.2 reshape.203
  388.9 0.6 gather_fusion
  389.5 0.8 fusion.7
  (9 shorter events, 0.1 us)
Async XLA Ops:
  6.5 4.4 %copy-start = (f32[1,16,4096]{2,1,0:T(8,128)S(1)}, f32[1,16,4096]{2,1,0:T(8,128)}, u32[]{:S(2)}) copy-start(f32[1,16,4096]{2,1,0:T(8,128)} %param.11) | copy-start | bytes 786436
  6.5 48.6 %all-gather.7.cloned.1.call-start = ((), (), s32[]{:S(2)}) async-start(), calls=%async_computation.2 | async-start | bytes 2359296 | tf_op jit(solution)/shard_map/all_gather | solution.py:74
  7.7 4.2 %copy-start.2 = (s32[1,16]{1,0:T(1,128)S(1)}, s32[1,16]{1,0:T(1,128)}, u32[]{:S(2)}) copy-start(s32[1,16]{1,0:T(1,128)} %param.12) | copy-start | bytes 196
  10.9 2.9 copy-start.1
  10.9 103.3 %all-gather.5.cloned.1.call-start = ((), (), s32[]{:S(2)}) async-start(), calls=%async_computation.1 | async-start | bytes 8650752 | tf_op jit(solution)/shard_map/all_gather | solution.py:78
  11.2 3.5 copy-start.3
  13.7 240.6 %all-gather.9.cloned.1.call-start = ((), (), s32[]{:S(2)}) async-start(), calls=%async_computation.3 | async-start | bytes 2359296 | tf_op jit(solution)/shard_map/all_gather | solution.py:75
  13.8 4.0 %copy-start.4 = (s32[1,16]{1,0:T(1,128)S(1)}, s32[1,16]{1,0:T(1,128)}, u32[]{:S(2)}) copy-start(s32[1,16]{1,0:T(1,128)} %param.20) | copy-start | bytes 196
  16.6 254.0 %all-gather.11.cloned.1.call-start = ((), (), s32[]{:S(2)}) async-start(), calls=%async_computation.4 | async-start | bytes 8650752 | tf_op jit(solution)/shard_map/all_gather | solution.py:93
  134.5 116.7 %all-to-all-start = ((f32[32,512,128]{1,2,0:T(8,128)}), f32[32,512,128]{1,2,0:T(8,128)}, u32[]{:S(2)}, u32[]{:S(2)}) async-start(f32[32,512,128]{1,2,0:T(8,128)} %stack.2), calls=%async_computation | async-start | bytes 16777216 | tf_op jit(solution)/shard_map/all_to_all | solution.py:84
  140.3 232.0 %all-reduce.2.cloned.1.call-start = ((), (), s32[]{:S(2)}) async-start(), calls=%async_computation.5 | async-start | bytes 4194304 | tf_op jit(solution)/shard_map/psum | solution.py:12
Sparse Core Ops, SparseCore 0:
  11.0 44.0 all-gather.6
  57.7 56.4 all-gather.4
  116.0 40.7 all-gather.8
  159.2 111.3 all-gather.10
  272.8 99.5 all-reduce.1
